TPU v7x, 32 devices: a whole 2x2x4 slice. The times are simulated.
32 devices in a mesh: dp: 8 (over z, y), mp: 4 (over x, core).
Axes of the slice: x: 2, y: 2, z: 4, core: 2. Of those that a mesh axis runs over, the one named last changes fastest.
Arguments:
- tokens: bfloat16 [32, 256, 1152], P('dp'), may hold values from -6 to 6
- condition: bfloat16 [32, 1152], P('dp'), may hold values from -6 to 6
- cotangent: bfloat16 [32, 256, 1152], P('dp'), may hold values from -12 to 12
- kept_index: int32 [32, 128], P('dp'), may hold values from 0 to 255, as said below
- skip_index: int32 [32, 128], P('dp'), may hold values from 0 to 255, as said below
- step_count: int32 [1], replicated, may hold values from 1 to 20
- ada_weight: float32 [1152, 6, 1152], P('dp', None, 'mp'), may hold values from -0.1875 to 0.1875
- qkv_weight: float32 [3, 1152, 1152], P(None, 'dp', 'mp'), may hold values from -0.1875 to 0.1875
- proj_weight: float32 [1152, 1152], P('mp', 'dp'), may hold values from -1 to 1
- fc1_weight: float32 [1152, 4608], P('dp', 'mp'), may hold values from -0.1875 to 0.1875
- fc2_weight: float32 [4608, 1152], P('mp', 'dp'), may hold values from -0.09375 to 0.09375
- ada_moment: float32 [1152, 6, 1152], P('dp', None, 'mp'), may hold values from -80 to 80
- qkv_moment: float32 [3, 1152, 1152], P(None, 'dp', 'mp'), may hold values from -80 to 80
- proj_moment: float32 [1152, 1152], P('mp', 'dp'), may hold values from -80 to 80
- fc1_moment: float32 [1152, 4608], P('dp', 'mp'), may hold values from -80 to 80
- fc2_moment: float32 [4608, 1152], P('mp', 'dp'), may hold values from -80 to 80
- ada_average: float32 [1152, 6, 1152], P('dp', None, 'mp'), may hold values from -0.1875 to 0.1875
- qkv_average: float32 [3, 1152, 1152], P(None, 'dp', 'mp'), may hold values from -0.1875 to 0.1875
- proj_average: float32 [1152, 1152], P('mp', 'dp'), may hold values from -1 to 1
- fc1_average: float32 [1152, 4608], P('dp', 'mp'), may hold values from -0.1875 to 0.1875
- fc2_average: float32 [4608, 1152], P('mp', 'dp'), may hold values from -0.09375 to 0.09375
Outputs:
- block_out: bfloat16 [32, 256, 1152], P('dp')
- tokens_grad: float32 [32, 256, 1152], P('dp')
- condition_grad: float32 [32, 1152], P('dp')
- ada_master: float32 [1152, 6, 1152], P('dp', None, 'mp')
- qkv_master: float32 [3, 1152, 1152], P(None, 'dp', 'mp')
- proj_master: float32 [1152, 1152], P('mp', 'dp')
- fc1_master: float32 [1152, 4608], P('dp', 'mp')
- fc2_master: float32 [4608, 1152], P('mp', 'dp')
- ada_momentum: float32 [1152, 6, 1152], P('dp', None, 'mp')
- qkv_momentum: float32 [3, 1152, 1152], P(None, 'dp', 'mp')
- proj_momentum: float32 [1152, 1152], P('mp', 'dp')
- fc1_momentum: float32 [1152, 4608], P('dp', 'mp')
- fc2_momentum: float32 [4608, 1152], P('mp', 'dp')
- ada_ema: float32 [1152, 6, 1152], P('dp', None, 'mp')
- qkv_ema: float32 [3, 1152, 1152], P(None, 'dp', 'mp')
- proj_ema: float32 [1152, 1152], P('mp', 'dp')
- fc1_ema: float32 [1152, 4608], P('dp', 'mp')
- fc2_ema: float32 [4608, 1152], P('mp', 'dp')
Inputs may be any that keep to these rules, and one draw needn't show every extreme that they name: `kept_index`: row b lists 128 distinct positions of image b in increasing order; row b of skip_index lists the other 128 positions in increasing order. `skip_index`: row b lists the positions of image b that kept_index does not, in increasing order.
All inputs are finite; a program needn't handle non-finite values.
Results may differ from a plain program's by a relative error of at most 0.012.
The roundings to bfloat16 on the way count: a program that leaves them out, or rounds other values in their place, can miss the bound.
Values may be sent and summed in bfloat16 or wider, within the bound.
No kernel may reach another device: no remote copies, remote signals or barrier semaphores. Data moves between devices by JAX's collectives and lax.ppermute only.
A program may use at most 192 MiB of HBM per device.

v0:
```python
from functools import partial
import math
import jax
import jax.numpy as jnp
from jax import lax
from jax.sharding import PartitionSpec as P

HEAD_DIM = 72
epsilon = 1e-06
momentum_rate = 0.9


def layer_norm(values):
    centered = values - jnp.mean(values, axis=-1, keepdims=True)
    inverse = lax.rsqrt(jnp.mean(centered * centered, axis=-1, keepdims=True) + epsilon)
    return (centered * inverse, inverse)


def norm_back(normed, inverse, gradient):
    return inverse * (
        gradient
        - jnp.mean(gradient, axis=-1, keepdims=True)
        - normed * jnp.mean(gradient * normed, axis=-1, keepdims=True)
    )


def pick_rows(values, index):
    return jnp.take_along_axis(values, index[:, :, None], axis=1)


def place_rows(kept_rows, other_rows, kept_index, skip_index):
    images = kept_index.shape[0]
    batch = jnp.arange(images, dtype=jnp.int32)[:, None]
    blank = jnp.zeros(
        (images, kept_index.shape[1] + skip_index.shape[1], kept_rows.shape[2]), kept_rows.dtype
    )
    return blank.at[batch, kept_index].set(kept_rows).at[batch, skip_index].set(other_rows)


def share_rows(values):
    return lax.psum_scatter(values, "mp", scatter_dimension=1, tiled=True)


def whole_rows(values):
    return lax.all_gather(values, "mp", axis=1, tiled=True)


def per_device(
    tokens,
    condition,
    cotangent,
    kept_index,
    skip_index,
    step_count,
    ada_weight,
    qkv_weight,
    proj_weight,
    fc1_weight,
    fc2_weight,
    ada_moment,
    qkv_moment,
    proj_moment,
    fc1_moment,
    fc2_moment,
    ada_average,
    qkv_average,
    proj_average,
    fc1_average,
    fc2_average,
):
    f32 = jnp.float32
    bf16 = jnp.bfloat16
    ada_low = ada_weight.astype(bf16)
    qkv_low = qkv_weight.astype(bf16)
    proj_low = proj_weight.astype(bf16)
    fc1_low = fc1_weight.astype(bf16)
    fc2_low = fc2_weight.astype(bf16)
    ada_full, qkv_full, proj_full, fc1_full, fc2_full = (
        lax.all_gather(ada_low, "dp", axis=0, tiled=True),
        lax.all_gather(qkv_low, "dp", axis=1, tiled=True),
        lax.all_gather(proj_low, "dp", axis=1, tiled=True),
        lax.all_gather(fc1_low, "dp", axis=0, tiled=True),
        lax.all_gather(fc2_low, "dp", axis=1, tiled=True),
    )
    images = tokens.shape[0]
    kept_count = kept_index.shape[1]
    local_width = qkv_full.shape[2]
    local_heads = local_width // HEAD_DIM
    score_scale = HEAD_DIM ** (-0.5)
    row_share = kept_count // lax.axis_size("mp")
    row_start = lax.axis_index("mp") * row_share

    def own_rows(values):
        return lax.dynamic_slice_in_dim(values, row_start, row_share, 1)

    cond_float = condition.astype(f32)
    silu_cond = jax.nn.silu(cond_float).astype(bf16)
    mod_part = jnp.einsum("bd,dkf->bkf", silu_cond, ada_full, preferred_element_type=f32)
    modulation = lax.all_gather(mod_part, "mp", axis=2, tiled=True)
    shift_one = modulation[:, 0, None, :]
    scale_one = modulation[:, 1, None, :]
    gate_one = modulation[:, 2, None, :]
    shift_two = modulation[:, 3, None, :]
    scale_two = modulation[:, 4, None, :]
    gate_two = modulation[:, 5, None, :]
    kept_rows = pick_rows(tokens, kept_index).astype(f32)
    normed_one, inverse_one = layer_norm(kept_rows)
    hidden = (normed_one * (1.0 + scale_one) + shift_one).astype(bf16)
    projected = jnp.einsum("bnd,tdf->tbnf", hidden, qkv_full, preferred_element_type=f32).astype(
        bf16
    )
    split_heads = projected.reshape(3, images, kept_count, local_heads, HEAD_DIM)
    query_heads = split_heads[0]
    key_heads = split_heads[1]
    value_heads = split_heads[2]
    scores = (
        jnp.einsum("bqhe,bkhe->bhqk", query_heads, key_heads, preferred_element_type=f32)
        * score_scale
    )
    row_max = jnp.max(scores, axis=-1, keepdims=True)
    exp_scores = jnp.exp(scores - row_max)
    row_total = jnp.sum(exp_scores, axis=-1, keepdims=True)
    log_total = row_max + jnp.log(row_total)
    probs = exp_scores / row_total
    attended = (
        jnp.einsum("bhqk,bkhe->bqhe", probs.astype(bf16), value_heads, preferred_element_type=f32)
        .astype(bf16)
        .reshape(images, kept_count, local_width)
    )
    attn_part = jnp.einsum("bnf,fd->bnd", attended, proj_full, preferred_element_type=f32)
    attn_out = share_rows(attn_part)
    residual = own_rows(kept_rows) + gate_one * attn_out
    normed_two, inverse_two = layer_norm(residual)
    hidden_two = whole_rows((normed_two * (1.0 + scale_two) + shift_two).astype(bf16))
    pre_act = jnp.einsum("bnd,df->bnf", hidden_two, fc1_full, preferred_element_type=f32)
    activated = jax.nn.gelu(pre_act, approximate=True).astype(bf16)
    mlp_part = jnp.einsum("bnf,fd->bnd", activated, fc2_full, preferred_element_type=f32)
    mlp_out = share_rows(mlp_part)
    kept_out = residual + gate_two * mlp_out
    kept_low = whole_rows(kept_out.astype(bf16))
    block_out = place_rows(kept_low, pick_rows(tokens, skip_index), kept_index, skip_index)
    ada_back, qkv_back, proj_back, fc1_back, fc2_back = (
        lax.all_gather(ada_low, "dp", axis=0, tiled=True),
        lax.all_gather(qkv_low, "dp", axis=1, tiled=True),
        lax.all_gather(proj_low, "dp", axis=1, tiled=True),
        lax.all_gather(fc1_low, "dp", axis=0, tiled=True),
        lax.all_gather(fc2_low, "dp", axis=1, tiled=True),
    )
    grad_float = cotangent.astype(f32)
    grad_kept = pick_rows(grad_float, kept_index)
    grad_here = own_rows(grad_kept)
    gate_two_grad = jnp.sum(grad_here * mlp_out, axis=1)
    mlp_out_grad = (gate_two * grad_kept).astype(bf16)
    fc2_grad = jnp.einsum("bnf,bnd->fd", activated, mlp_out_grad, preferred_element_type=f32)
    act_grad = jnp.einsum("bnd,fd->bnf", mlp_out_grad, fc2_back, preferred_element_type=f32)
    gelu_value, gelu_pull = jax.vjp(partial(jax.nn.gelu, approximate=True), pre_act)
    pre_grad = gelu_pull(act_grad)[0].astype(bf16)
    fc1_grad = jnp.einsum("bnd,bnf->df", hidden_two, pre_grad, preferred_element_type=f32)
    hidden_two_part = jnp.einsum("bnf,df->bnd", pre_grad, fc1_back, preferred_element_type=f32)
    hidden_two_grad = share_rows(hidden_two_part)
    shift_two_grad = jnp.sum(hidden_two_grad, axis=1)
    scale_two_grad = jnp.sum(hidden_two_grad * normed_two, axis=1)
    residual_grad = grad_here + norm_back(
        normed_two, inverse_two, hidden_two_grad * (1.0 + scale_two)
    )
    gate_one_grad = jnp.sum(residual_grad * attn_out, axis=1)
    attn_out_grad = whole_rows((gate_one * residual_grad).astype(bf16))
    proj_grad = jnp.einsum("bnf,bnd->fd", attended, attn_out_grad, preferred_element_type=f32)
    attended_grad = jnp.einsum(
        "bnd,fd->bnf", attn_out_grad, proj_back, preferred_element_type=f32
    ).astype(bf16)
    attended_grad = attended_grad.reshape(images, kept_count, local_heads, HEAD_DIM)
    again_scores = (
        jnp.einsum("bqhe,bkhe->bhqk", query_heads, key_heads, preferred_element_type=f32)
        * score_scale
    )
    again_probs = jnp.exp(again_scores - log_total)
    prob_grad = jnp.einsum(
        "bqhe,bkhe->bhqk", attended_grad, value_heads, preferred_element_type=f32
    )
    score_grad = (
        again_probs * (prob_grad - jnp.sum(prob_grad * again_probs, axis=-1, keepdims=True))
    ).astype(bf16)
    query_grad = (
        jnp.einsum("bhqk,bkhe->bqhe", score_grad, key_heads, preferred_element_type=f32)
        * score_scale
    )
    key_grad = (
        jnp.einsum("bhqk,bqhe->bkhe", score_grad, query_heads, preferred_element_type=f32)
        * score_scale
    )
    value_grad = jnp.einsum(
        "bhqk,bqhe->bkhe", again_probs.astype(bf16), attended_grad, preferred_element_type=f32
    )
    grad_rows = (
        jnp.stack([query_grad, key_grad, value_grad])
        .astype(bf16)
        .reshape(3, images, kept_count, local_width)
    )
    qkv_grad = jnp.einsum("tbnf,bnd->tdf", grad_rows, hidden, preferred_element_type=f32)
    hidden_part = jnp.einsum("tbnf,tdf->bnd", grad_rows, qkv_back, preferred_element_type=f32)
    hidden_grad = share_rows(hidden_part)
    normed_here = own_rows(normed_one)
    inverse_here = own_rows(inverse_one)
    shift_one_grad = jnp.sum(hidden_grad, axis=1)
    scale_one_grad = jnp.sum(hidden_grad * normed_here, axis=1)
    kept_share = residual_grad + norm_back(
        normed_here, inverse_here, hidden_grad * (1.0 + scale_one)
    )
    kept_grad = lax.all_gather(kept_share, "mp", axis=1, tiled=True)
    tokens_grad = place_rows(kept_grad, pick_rows(grad_float, skip_index), kept_index, skip_index)
    mod_grad = jnp.stack(
        [
            shift_one_grad,
            scale_one_grad,
            gate_one_grad,
            shift_two_grad,
            scale_two_grad,
            gate_two_grad,
        ],
        axis=1,
    )
    mod_local = lax.psum_scatter(mod_grad, "mp", scatter_dimension=2, tiled=True).astype(bf16)
    ada_grad = jnp.einsum("bd,bkf->dkf", silu_cond, mod_local, preferred_element_type=f32)
    silu_grad = lax.psum(
        jnp.einsum("bkf,dkf->bd", mod_local, ada_back, preferred_element_type=f32), "mp"
    )
    silu_value, silu_pull = jax.vjp(jax.nn.silu, cond_float)
    condition_grad = silu_pull(silu_grad)[0]
    ada_shard, qkv_shard, proj_shard, fc1_shard, fc2_shard = (
        lax.psum_scatter(ada_grad, "dp", scatter_dimension=0, tiled=True),
        lax.psum_scatter(qkv_grad, "dp", scatter_dimension=1, tiled=True),
        lax.psum_scatter(proj_grad, "dp", scatter_dimension=1, tiled=True),
        lax.psum_scatter(fc1_grad, "dp", scatter_dimension=0, tiled=True),
        lax.psum_scatter(fc2_grad, "dp", scatter_dimension=1, tiled=True),
    )
    rate = 0.02 / math.sqrt(images * lax.axis_size("dp") * kept_count)
    step_float = step_count.astype(f32)[0]
    decay = (1.0 + step_float) / (10.0 + step_float)

    def update(weight, moment, average, gradient):
        new_moment = momentum_rate * moment + gradient
        master = weight - rate * (gradient + momentum_rate * new_moment)
        return (master, new_moment, decay * average + (1.0 - decay) * master)

    ada_master, ada_momentum, ada_ema = update(ada_weight, ada_moment, ada_average, ada_shard)
    qkv_master, qkv_momentum, qkv_ema = update(qkv_weight, qkv_moment, qkv_average, qkv_shard)
    proj_master, proj_momentum, proj_ema = update(
        proj_weight, proj_moment, proj_average, proj_shard
    )
    fc1_master, fc1_momentum, fc1_ema = update(fc1_weight, fc1_moment, fc1_average, fc1_shard)
    fc2_master, fc2_momentum, fc2_ema = update(fc2_weight, fc2_moment, fc2_average, fc2_shard)
    return (
        block_out,
        tokens_grad,
        condition_grad,
        ada_master,
        qkv_master,
        proj_master,
        fc1_master,
        fc2_master,
        ada_momentum,
        qkv_momentum,
        proj_momentum,
        fc1_momentum,
        fc2_momentum,
        ada_ema,
        qkv_ema,
        proj_ema,
        fc1_ema,
        fc2_ema,
    )


def solution(mesh):
    placed = (
        P("dp", None, None),
        P("dp", None),
        P("dp", None, None),
        P("dp", None),
        P("dp", None),
        P(),
        P("dp", None, "mp"),
        P(None, "dp", "mp"),
        P("mp", "dp"),
        P("dp", "mp"),
        P("mp", "dp"),
        P("dp", None, "mp"),
        P(None, "dp", "mp"),
        P("mp", "dp"),
        P("dp", "mp"),
        P("mp", "dp"),
        P("dp", None, "mp"),
        P(None, "dp", "mp"),
        P("mp", "dp"),
        P("dp", "mp"),
        P("mp", "dp"),
    )
    return jax.shard_map(
        per_device,
        mesh=mesh,
        in_specs=placed,
        out_specs=(
            P("dp", None, None),
            P("dp", None, None),
            P("dp", None),
            P("dp", None, "mp"),
            P(None, "dp", "mp"),
            P("mp", "dp"),
            P("dp", "mp"),
            P("mp", "dp"),
            P("dp", None, "mp"),
            P(None, "dp", "mp"),
            P("mp", "dp"),
            P("dp", "mp"),
            P("mp", "dp"),
            P("dp", None, "mp"),
            P(None, "dp", "mp"),
            P("mp", "dp"),
            P("dp", "mp"),
            P("mp", "dp"),
        ),
        check_vma=False,
    )
```

profile of v0, /device:TPU:0, one launch (start us, length us, event | category | flops | bytes accessed | tf_op | source)
XLA Modules:
  0.0 1142.5 jit_solution(12994166128726137092)
XLA Ops:
  11.3 5.7 gather_fusion
  18.1 38.6 %all_gather.38 = bf16[288,1152]{0,1:T(8,128)(2,1)} all-gather(bf16[288,144]{0,1:T(8,128)(2,1)S(1)} %copy-done.21), channel_id=1, replica_groups=mesh['dp'=8,'mp'=4] {'dp'}, dimensions={1}, use_global_device_ids=true | all-gather | bytes 746496 | tf_op jit(solution)/shard_map/all_gather | solution.py:81
  56.7 51.9 %all-gather.9.cloned.1.call-done = bf16[1152,6,288]{2,0,1:T(8,128)(2,1)} async-done(((bf16[144,6,288]{2,0,1:T(8,128)(2,1)}), bf16[1152,6,288]{2,0,1:T(8,128)(2,1)}) %all-gather.9.cloned.1.call-update) | async-done | bytes 3981328 | tf_op jit(solution)/shard_map/all_gather | solution.py:79
  114.4 17.3 %all_gather.36 = f32[4,6,1152]{1,0,2:T(4,128)S(1)} all-gather(f32[4,6,288]{1,0,2:T(4,128)} %copy.115), channel_id=1, replica_groups=mesh['dp'=8,'mp'=4] {'mp'}, dimensions={2}, use_global_device_ids=true | all-gather | bytes 138240 | tf_op jit(solution)/shard_map/all_gather | solution.py:99
  131.7 9.2 fusion.74
  147.7 17.1 %all-gather.11.cloned.1.call-done = bf16[3,1152,288]{2,1,0:T(8,128)(2,1)} async-done(((bf16[3,144,288]{2,1,0:T(8,128)(2,1)}), bf16[3,1152,288]{2,1,0:T(8,128)(2,1)}) %all-gather.11.cloned.1.call-update) | async-done | bytes 1990672 | tf_op jit(solution)/shard_map/all_gather | solution.py:80
  186.2 18.3 %reduce-scatter.15.cloned.1.call-done = f32[4,32,1152]{2,1,0:T(8,128)} async-done(((f32[4,128,1152]{2,1,0:T(8,128)}), f32[4,32,1152]{2,1,0:T(8,128)}) %reduce-scatter.15.cloned.1.call-update) | async-done | bytes 589840 | tf_op jit(solution)/shard_map/reduce_scatter | solution.py:41
  212.0 11.0 gather_fusion.2
  230.0 32.5 %all-gather.15.cloned.1.call-done = bf16[1152,1152]{1,0:T(8,128)(2,1)} async-done(((bf16[144,1152]{1,0:T(8,128)(2,1)}), bf16[1152,1152]{1,0:T(8,128)(2,1)}) %all-gather.15.cloned.1.call-update) | async-done | bytes 2654224 | tf_op jit(solution)/shard_map/all_gather | solution.py:82
  262.5 18.1 %all-gather.13.cloned.1.call-done = bf16[4,128,1152]{2,1,0:T(8,128)(2,1)} async-done(((bf16[4,32,1152]{2,1,0:T(8,128)(2,1)}), bf16[4,128,1152]{2,1,0:T(8,128)(2,1)}) %all-gather.13.cloned.1.call-update) | async-done | bytes 1179664 | tf_op jit(solution)/shard_map/all_gather | solution.py:45
  291.1 103.6 %reduce-scatter.29.cloned.1.call-done = f32[1152,144]{0,1:T(8,128)} async-done(((f32[1152,1152]{0,1:T(8,128)}), f32[1152,144]{0,1:T(8,128)}) %reduce-scatter.29.cloned.1.call-update) | async-done | bytes 663568 | tf_op jit(solution)/shard_map/reduce_scatter | solution.py:235
  398.2 54.9 %all-gather.17.cloned.1.call-done = bf16[1152,1152]{0,1:T(8,128)(2,1)} async-done(((bf16[1152,144]{0,1:T(8,128)(2,1)}), bf16[1152,1152]{0,1:T(8,128)(2,1)}) %all-gather.17.cloned.1.call-update) | async-done | bytes 2654224 | tf_op jit(solution)/shard_map/all_gather | solution.py:83
  453.1 5.8 fusion.17
  463.6 6.1 fusion.2
  469.7 25.4 %reduce-scatter.19.cloned.1.call-done = f32[4,32,1152]{2,1,0:T(8,128)} async-done(((f32[4,128,1152]{2,1,0:T(8,128)}), f32[4,32,1152]{2,1,0:T(8,128)}) %reduce-scatter.19.cloned.1.call-update) | async-done | bytes 589840 | tf_op jit(solution)/shard_map/reduce_scatter | solution.py:41
  497.9 33.0 %reduce-scatter.17.cloned.1.call-done = f32[4,32,1152]{2,1,0:T(8,128)} async-done(((f32[4,128,1152]{2,1,0:T(8,128)}), f32[4,32,1152]{2,1,0:T(8,128)}) %reduce-scatter.17.cloned.1.call-update) | async-done | bytes 589840 | tf_op jit(solution)/shard_map/reduce_scatter | solution.py:41
  536.8 16.8 %all-gather.21.cloned.1.call-done = bf16[4,128,1152]{2,1,0:T(8,128)(2,1)} async-done(((bf16[4,32,1152]{2,1,0:T(8,128)(2,1)}), bf16[4,128,1152]{2,1,0:T(8,128)(2,1)}) %all-gather.21.cloned.1.call-update) | async-done | bytes 1179664 | tf_op jit(solution)/shard_map/all_gather | solution.py:45
  562.4 33.2 %reduce-scatter.21.cloned.1.call-done = f32[4,32,1152]{2,1,0:T(8,128)} async-done(((f32[4,128,1152]{2,1,0:T(8,128)}), f32[4,32,1152]{2,1,0:T(8,128)}) %reduce-scatter.21.cloned.1.call-update) | async-done | bytes 589840 | tf_op jit(solution)/shard_map/reduce_scatter | solution.py:41
  616.5 5.8 convolution_bitcast_fusion.1
  627.6 8.6 copy.147
  636.2 9.0 reshape.214
  651.3 5.7 fusion.46
  658.4 11.0 gather_fusion.3
  669.4 8.4 gather_fusion.1
  688.4 78.5 %scatter_fusion = bf16[4,256,1152]{2,1,0:T(8,128)(2,1)} fusion(bf16[4,256,1152]{2,1,0:T(8,128)(2,1)} %broadcast_in_dim.28, s32[512]{0:T(512)S(1)} %get-tuple-element.152, bf16[512,1152]{1,0:T(8,128)(2,1)} %bitcast.198), kind=kCustom, calls=%fused_computation.4 | custom fusion | bytes 3543040 | tf_op jit(solution)/shard_map/scatter | solution.py:37
  766.9 78.8 %scatter_fusion.1 = bf16[4,256,1152]{2,1,0:T(8,128)(2,1)} fusion(bf16[4,256,1152]{2,1,0:T(8,128)(2,1)} %scatter_fusion, s32[512]{0:T(512)S(1)} %get-tuple-element.150, bf16[512,1152]{1,0:T(8,128)(2,1)} %bitcast.187), kind=kCustom, calls=%fused_computation.5 | custom fusion | bytes 3543040 | tf_op jit(solution)/shard_map/scatter | solution.py:37
  854.9 11.2 psum.7
  866.8 55.1 %reduce-scatter.33.cloned.1.call-done = f32[144,864]{1,0:T(8,128)} async-done(((f32[1152,864]{1,0:T(8,128)}), f32[144,864]{1,0:T(8,128)}) %reduce-scatter.33.cloned.1.call-update) | async-done | bytes 497680
  936.3 10.9 all-gather.23.cloned.1.call-done
  949.7 80.0 %scatter_fusion.2 = f32[4,256,1152]{2,1,0:T(8,128)} fusion(f32[4,256,1152]{2,1,0:T(8,128)} %broadcast_in_dim.35, s32[512]{0:T(512)S(1)} %get-tuple-element.152, f32[512,1152]{1,0:T(8,128)} %bitcast.196), kind=kCustom, calls=%fused_computation.6 | custom fusion | bytes 7081984 | tf_op jit(solution)/shard_map/scatter | solution.py:37
  1029.7 79.8 %scatter_fusion.3 = f32[4,256,1152]{2,1,0:T(8,128)} fusion(f32[4,256,1152]{2,1,0:T(8,128)} %scatter_fusion.2, s32[512]{0:T(512)S(1)} %get-tuple-element.150, f32[512,1152]{1,0:T(8,128)} %bitcast.184), kind=kCustom, calls=%fused_computation.7 | custom fusion | bytes 7081984 | tf_op jit(solution)/shard_map/scatter | solution.py:37
  1109.5 21.1 %reduce-scatter.23.cloned.1.call-done = f32[144,6,288]{2,0,1:T(8,128)} async-done(((f32[1152,6,288]{2,0,1:T(8,128)}), f32[144,6,288]{2,0,1:T(8,128)}) %reduce-scatter.23.cloned.1.call-update) | async-done | bytes 995344 | tf_op jit(solution)/shard_map/reduce_scatter | solution.py:231
  (217 shorter events, 164.5 us)
Async XLA Ops:
  7.2 4.1 copy-start
  7.2 2.5 copy-start.14
  7.2 3.4 copy-start.19
  7.2 4.0 copy-start.39
  7.2 101.4 %all-gather.9.cloned.1.call-start = ((), (), s32[]{:S(2)}) async-start(), calls=%async_computation.10 | async-start | bytes 5971968 | tf_op jit(solution)/shard_map/all_gather | solution.py:79
  9.7 155.0 %all-gather.11.cloned.1.call-start = ((), (), s32[]{:S(2)}) async-start(), calls=%async_computation.11 | async-start | bytes 2985984 | tf_op jit(solution)/shard_map/all_gather | solution.py:80
  10.5 194.0 %reduce-scatter.15.cloned.1.call-start = ((), (), s32[]{:S(2)}) async-start(), calls=%async_computation.12 | async-start | bytes 2949120 | tf_op jit(solution)/shard_map/reduce_scatter | solution.py:41
  17.5 147.2 %copy-start.32 = (f32[4,128]{1,0:T(4,128)}, f32[4,128]{1,0:T(4,128)S(1)}, u32[]{:S(2)}) copy-start(f32[4,128]{1,0:T(4,128)S(1)} %broadcast_multiply_fusion.5) | copy-start | bytes 6148
  18.1 146.7 %copy-start.34 = (f32[4,128]{1,0:T(4,128)}, f32[4,128]{1,0:T(4,128)S(1)}, u32[]{:S(2)}) copy-start(f32[4,128]{1,0:T(4,128)S(1)} %add_rsqrt_fusion.1) | copy-start | bytes 6148
  172.8 89.7 %all-gather.15.cloned.1.call-start = ((), (), s32[]{:S(2)}) async-start(), calls=%async_computation.14 | async-start | bytes 2985984 | tf_op jit(solution)/shard_map/all_gather | solution.py:82
  174.7 105.9 %all-gather.13.cloned.1.call-start = ((), (), s32[]{:S(2)}) async-start(), calls=%async_computation.13 | async-start | bytes 1474560 | tf_op jit(solution)/shard_map/all_gather | solution.py:45
  207.8 186.9 %reduce-scatter.29.cloned.1.call-start = ((), (), s32[]{:S(2)}) async-start(), calls=%async_computation.25 | async-start | bytes 5971968 | tf_op jit(solution)/shard_map/reduce_scatter | solution.py:235
  280.6 5.5 copy-start.8
  280.6 5.5 copy-start.29
  290.4 162.7 %all-gather.17.cloned.1.call-start = ((), (), s32[]{:S(2)}) async-start(), calls=%async_computation.15 | async-start | bytes 2985984 | tf_op jit(solution)/shard_map/all_gather | solution.py:83
  398.2 97.0 %reduce-scatter.19.cloned.1.call-start = ((), (), s32[]{:S(2)}) async-start(), calls=%async_computation.18 | async-start | bytes 2949120 | tf_op jit(solution)/shard_map/reduce_scatter | solution.py:41
  453.1 6.8 copy-start.42
  463.3 67.6 %reduce-scatter.17.cloned.1.call-start = ((), (), s32[]{:S(2)}) async-start(), calls=%async_computation.16 | async-start | bytes 2949120 | tf_op jit(solution)/shard_map/reduce_scatter | solution.py:41
  469.7 83.9 %all-gather.21.cloned.1.call-start = ((), (), s32[]{:S(2)}) async-start(), calls=%async_computation.19 | async-start | bytes 1474560 | tf_op jit(solution)/shard_map/all_gather | solution.py:45
  530.9 4.3 copy-start.26
  536.0 59.6 %reduce-scatter.21.cloned.1.call-start = ((), (), s32[]{:S(2)}) async-start(), calls=%async_computation.20 | async-start | bytes 2949120 | tf_op jit(solution)/shard_map/reduce_scatter | solution.py:41
  562.4 87.2 %reduce-scatter.31.cloned.1.call-start = ((), (), s32[]{:S(2)}) async-start(), calls=%async_computation.26 | async-start | bytes 737280
  612.2 74.7 %all-gather.19.cloned.1.call-start = ((), (), s32[]{:S(2)}) async-start(), calls=%async_computation.17 | async-start | bytes 1474560 | tf_op jit(solution)/shard_map/all_gather | solution.py:45
  612.9 232.7 %reduce-scatter.25.cloned.1.call-start = ((), (), s32[]{:S(2)}) async-start(), calls=%async_computation.23 | async-start | bytes 1990656 | tf_op jit(solution)/shard_map/reduce_scatter | solution.py:233
  616.4 231.3 %reduce-scatter.27.cloned.1.call-start = ((), (), s32[]{:S(2)}) async-start(), calls=%async_computation.24 | async-start | bytes 5971968 | tf_op jit(solution)/shard_map/reduce_scatter | solution.py:234
  622.3 299.6 %reduce-scatter.33.cloned.1.call-start = ((), (), s32[]{:S(2)}) async-start(), calls=%async_computation.27 | async-start | bytes 4644864
  645.2 6.0 copy-start.27
  645.2 302.0 %all-gather.23.cloned.1.call-start = ((), (), s32[]{:S(2)}) async-start(), calls=%async_computation.21 | async-start | bytes 2949120 | tf_op jit(solution)/shard_map/all_gather | solution.py:210
  649.6 481.1 %reduce-scatter.23.cloned.1.call-start = ((), (), s32[]{:S(2)}) async-start(), calls=%async_computation.22 | async-start | bytes 11943936 | tf_op jit(solution)/shard_map/reduce_scatter | solution.py:231
  682.5 2.7 copy-start.4
  766.9 78.8 %copy-start.20 = (f32[288,144]{0,1:T(8,128)S(1)}, f32[288,144]{0,1:T(8,128)}, u32[]{:S(2)}) copy-start(f32[288,144]{0,1:T(8,128)} %param.33) | copy-start | bytes 497668
  930.2 4.9 copy-start.9
  (31 other events, 38.8 us)
Sparse Core Ops, SparseCore 0:
  10.9 97.7 all-gather.8
  111.5 53.2 all-gather.10
  172.9 31.5 reduce-scatter.14
  207.4 55.0 all-gather.14
  264.5 16.0 all-gather.12
  290.5 104.1 reduce-scatter.28
  398.3 54.7 all-gather.16
  463.4 31.6 reduce-scatter.18
  497.8 33.0 reduce-scatter.16
  536.1 17.4 all-gather.20
  562.5 33.0 reduce-scatter.20
  612.3 22.0 reduce-scatter.30
  636.6 17.4 all-gather.18
  657.8 66.3 reduce-scatter.24
  727.6 102.9 reduce-scatter.26
  834.5 87.4 reduce-scatter.32
  923.3 23.8 all-gather.22
  950.6 179.9 reduce-scatter.22
where the time goes:
time: 1160 us; the launch traced here: 1140 us
  waiting for transfers between devices  493 us (42%)
  local copies, waits for them, and re-layouts  442 us (38%)
  blocking collectives  67.2 us (6%)
  matrix products  65 us (6%)
  other arithmetic  57.6 us (5%)
  between operations  15.7 us (1%)
    scatter x4, local copies, waits for them, and re-layouts, place_rows(): blank.at[batch, kept_index].set(kept_rows).at[batch, skip_index]  317 us
    reduce_scatter x4, waiting for transfers between devices, share_rows(): return lax.psum_scatter(values, 'mp', scatter_dimension=1, tiled=True)  110 us
    reduce_scatter x1, waiting for transfers between devices, per_device(): lax.psum_scatter(fc2_grad, 'dp', scatter_dimension=1, tiled=True)  104 us
    unnamed x111, local copies, waits for them, and re-layouts  61.3 us
    unnamed x20, waiting for transfers between devices  56.1 us
    all_gather x1, waiting for transfers between devices, per_device(): lax.all_gather(fc2_low, 'dp', axis=1, tiled=True)  54.9 us
    all_gather x1, waiting for transfers between devices, per_device(): lax.all_gather(ada_low, 'dp', axis=0, tiled=True)  51.9 us
    all_gather x1, blocking collectives, per_device(): lax.all_gather(proj_low, 'dp', axis=1, tiled=True)  38.6 us
  transfers between devices with their start and end apart: 18, of which 14 were waited for; matrix products, arithmetic and copies ran while one was open for 43% of the time, Pallas kernels for 0%

commit v1 on v0

--- a/solution.py
+++ b/solution.py
@@ -1,3 +1,4 @@
+import functools
 from functools import partial
 import math
 import jax
@@ -8,6 +9,37 @@
 HEAD_DIM = 72
 epsilon = 1e-06
 momentum_rate = 0.9
+
+
+def refer_the_kinds(array_here, dimension_no):
+    y_new = list(array_here.shape[1:])
+    y_new[dimension_no] *= array_here.shape[0]
+    return jnp.moveaxis(array_here, 0, dimension_no).reshape(y_new)
+
+
+def lay_groups(xin, along_axis, array_axis):
+    store = []
+    n_dev_all = lax.psum(1, axis_name=along_axis)
+    for num in range(n_dev_all):
+        store.append((num, (num + 1) % n_dev_all))
+    panels = []
+    for at, rr in store:
+        panels.append((rr, at))
+    w2, newest = ([], [])
+    for dev_j in range(n_dev_all - 1):
+        if dev_j % 2 == 0:
+            w2.append(lax.ppermute(w2[-1] if w2 else xin, axis_name=along_axis, perm=store))
+        else:
+            newest.append(
+                lax.ppermute(newest[-1] if newest else xin, axis_name=along_axis, perm=panels)
+            )
+    val = jnp.stack([*w2[::-1], xin, *newest])
+    later = lax.axis_index(along_axis) - len(w2)
+    val = val[(jnp.arange(n_dev_all) - later) % n_dev_all]
+    return refer_the_kinds(val, array_axis)
+
+
+_advance_block = functools.partial(lay_groups, along_axis="dp", array_axis=0)
 
 
 def layer_norm(values):
@@ -79,7 +111,7 @@
         lax.all_gather(ada_low, "dp", axis=0, tiled=True),
         lax.all_gather(qkv_low, "dp", axis=1, tiled=True),
         lax.all_gather(proj_low, "dp", axis=1, tiled=True),
-        lax.all_gather(fc1_low, "dp", axis=0, tiled=True),
+        _advance_block(fc1_low),
         lax.all_gather(fc2_low, "dp", axis=1, tiled=True),
     )
     images = tokens.shape[0]

time: 1160 us -> 1210 us (1.043)
  local copies, waits for them, and re-layouts: 442 us -> 458 us
  starting transfers between devices: 1.53 us -> 15.5 us
    ppermute x0 -> x7, waiting for transfers between devices: none -> 25.2 us  [the longest x4 24.2 us: lay_groups(): lax.ppermute(w2[-1] if w2 else xin, axis_name=along_axis, perm=store)]
    reduce_scatter x4, waiting for transfers between devices: 110 us -> 91.5 us  [share_rows(): return lax.psum_scatter(values, 'mp', scatter_dimension=1, tiled=True)]
    all_gather x1, waiting for transfers between devices: 32.5 us -> 49.7 us  [per_device(): lax.all_gather(fc1_low, 'dp', axis=0, tiled=True)]
    all_gather x3, waiting for transfers between devices: 35 us -> 19.3 us  [whole_rows(): return lax.all_gather(values, 'mp', axis=1, tiled=True)]
    ppermute x0 -> x7, starting transfers between devices: none -> 13.8 us  [the longest x3 10.8 us: lay_groups(): lax.ppermute(newest[-1] if newest else xin, axis_name=along_axis, perm=pa...]
    unnamed x111 -> x125, local copies, waits for them, and re-layouts: 61.3 us -> 70.9 us
  transfers between devices with their start and end apart: 18 -> 25, of which waited for: 14 -> 17; matrix products, arithmetic and copies ran while one was open for 43% -> 44% of each run, Pallas kernels for 0% -> 0%
where the time goes in v1:
time: 1210 us; the launch traced here: 1190 us
  waiting for transfers between devices  501 us (41%)
  local copies, waits for them, and re-layouts  458 us (38%)
  matrix products  67.9 us (6%)
  blocking collectives  67.3 us (6%)
  other arithmetic  59.8 us (5%)
  between operations  15.7 us (1%)
  starting transfers between devices  15.5 us (1%)
    scatter x4, local copies, waits for them, and re-layouts, place_rows(): blank.at[batch, kept_index].set(kept_rows).at[batch, skip_index]  317 us
    reduce_scatter x1, waiting for transfers between devices, per_device(): lax.psum_scatter(fc2_grad, 'dp', scatter_dimension=1, tiled=True)  104 us
    reduce_scatter x4, waiting for transfers between devices, share_rows(): return lax.psum_scatter(values, 'mp', scatter_dimension=1, tiled=True)  91.5 us
    unnamed x125, local copies, waits for them, and re-layouts  70.9 us
    unnamed x20, waiting for transfers between devices  56.9 us
    all_gather x1, waiting for transfers between devices, per_device(): lax.all_gather(fc2_low, 'dp', axis=1, tiled=True)  53.9 us
    all_gather x1, waiting for transfers between devices, per_device(): lax.all_gather(ada_low, 'dp', axis=0, tiled=True)  51.9 us
    all_gather x1, waiting for transfers between devices, per_device(): lax.all_gather(fc1_low, 'dp', axis=0, tiled=True)  49.7 us
  transfers between devices with their start and end apart: 25, of which 17 were waited for; matrix products, arithmetic and copies ran while one was open for 44% of the time, Pallas kernels for 0%

profile of v1, /device:TPU:0, one launch (start us, length us, event | category | flops | bytes accessed | tf_op | source)
XLA Modules:
  0.0 1185.5 jit_solution(16585765767043949789)
XLA Ops:
  11.3 5.7 gather_fusion.1
  18.1 38.6 %all_gather.37 = bf16[288,1152]{0,1:T(8,128)(2,1)} all-gather(bf16[288,144]{0,1:T(8,128)(2,1)S(1)} %copy-done.25), channel_id=1, replica_groups=mesh['dp'=8,'mp'=4] {'dp'}, dimensions={1}, use_global_device_ids=true | all-gather | bytes 746496 | tf_op jit(solution)/shard_map/all_gather | solution.py:113
  56.7 51.9 %all-gather.9.cloned.1.call-done = bf16[1152,6,288]{2,0,1:T(8,128)(2,1)} async-done(((bf16[144,6,288]{2,0,1:T(8,128)(2,1)}), bf16[1152,6,288]{2,0,1:T(8,128)(2,1)}) %all-gather.9.cloned.1.call-update) | async-done | bytes 3981328 | tf_op jit(solution)/shard_map/all_gather | solution.py:111
  114.4 17.3 %all_gather.35 = f32[4,6,1152]{1,0,2:T(4,128)S(1)} all-gather(f32[4,6,288]{1,0,2:T(4,128)} %copy.115), channel_id=1, replica_groups=mesh['dp'=8,'mp'=4] {'mp'}, dimensions={2}, use_global_device_ids=true | all-gather | bytes 138240 | tf_op jit(solution)/shard_map/all_gather | solution.py:131
  131.7 9.2 fusion.74
  147.6 17.1 %all-gather.11.cloned.1.call-done = bf16[3,1152,288]{2,1,0:T(8,128)(2,1)} async-done(((bf16[3,144,288]{2,1,0:T(8,128)(2,1)}), bf16[3,1152,288]{2,1,0:T(8,128)(2,1)}) %all-gather.11.cloned.1.call-update) | async-done | bytes 1990672 | tf_op jit(solution)/shard_map/all_gather | solution.py:112
  175.3 10.7 collective-permute-done
  195.0 11.1 gather_fusion.3
  215.1 5.9 collective-permute-done.2
  228.1 7.5 collective-permute-done.3
  282.3 103.6 %reduce-scatter.29.cloned.1.call-done = f32[1152,144]{0,1:T(8,128)} async-done(((f32[1152,1152]{0,1:T(8,128)}), f32[1152,144]{0,1:T(8,128)}) %reduce-scatter.29.cloned.1.call-update) | async-done | bytes 663568 | tf_op jit(solution)/shard_map/reduce_scatter | solution.py:267
  390.4 53.9 %all-gather.15.cloned.1.call-done = bf16[1152,1152]{0,1:T(8,128)(2,1)} async-done(((bf16[1152,144]{0,1:T(8,128)(2,1)}), bf16[1152,1152]{0,1:T(8,128)(2,1)}) %all-gather.15.cloned.1.call-update) | async-done | bytes 2654224 | tf_op jit(solution)/shard_map/all_gather | solution.py:115
  444.3 6.7 fusion.15
  451.0 49.7 %all-gather.19.cloned.1.call-done = bf16[1152,1152]{1,0:T(8,128)(2,1)} async-done(((bf16[144,1152]{1,0:T(8,128)(2,1)}), bf16[1152,1152]{1,0:T(8,128)(2,1)}) %all-gather.19.cloned.1.call-update) | async-done | bytes 2654224 | tf_op jit(solution)/shard_map/all_gather | solution.py:178
  506.2 6.1 fusion.4
  512.3 25.6 %reduce-scatter.19.cloned.1.call-done = f32[4,32,1152]{2,1,0:T(8,128)} async-done(((f32[4,128,1152]{2,1,0:T(8,128)}), f32[4,32,1152]{2,1,0:T(8,128)}) %reduce-scatter.19.cloned.1.call-update) | async-done | bytes 589840 | tf_op jit(solution)/shard_map/reduce_scatter | solution.py:73
  540.7 33.0 %reduce-scatter.17.cloned.1.call-done = f32[4,32,1152]{2,1,0:T(8,128)} async-done(((f32[4,128,1152]{2,1,0:T(8,128)}), f32[4,32,1152]{2,1,0:T(8,128)}) %reduce-scatter.17.cloned.1.call-update) | async-done | bytes 589840 | tf_op jit(solution)/shard_map/reduce_scatter | solution.py:73
  579.6 16.8 %all-gather.21.cloned.1.call-done = bf16[4,128,1152]{2,1,0:T(8,128)(2,1)} async-done(((bf16[4,32,1152]{2,1,0:T(8,128)(2,1)}), bf16[4,128,1152]{2,1,0:T(8,128)(2,1)}) %all-gather.21.cloned.1.call-update) | async-done | bytes 1179664 | tf_op jit(solution)/shard_map/all_gather | solution.py:77
  605.5 32.9 %reduce-scatter.21.cloned.1.call-done = f32[4,32,1152]{2,1,0:T(8,128)} async-done(((f32[4,128,1152]{2,1,0:T(8,128)}), f32[4,32,1152]{2,1,0:T(8,128)}) %reduce-scatter.21.cloned.1.call-update) | async-done | bytes 589840 | tf_op jit(solution)/shard_map/reduce_scatter | solution.py:73
  659.2 5.7 convolution_bitcast_fusion.1
  670.3 8.6 copy.147
  678.9 9.0 reshape.276
  702.5 10.8 gather_fusion.4
  713.4 8.4 gather_fusion.2
  731.4 78.5 %scatter_fusion = bf16[4,256,1152]{2,1,0:T(8,128)(2,1)} fusion(bf16[4,256,1152]{2,1,0:T(8,128)(2,1)} %broadcast_in_dim.26, s32[512]{0:T(512)S(1)} %get-tuple-element.152, bf16[512,1152]{1,0:T(8,128)(2,1)} %bitcast.219), kind=kCustom, calls=%fused_computation.5 | custom fusion | bytes 3543040 | tf_op jit(solution)/shard_map/scatter | solution.py:69
  809.9 78.8 %scatter_fusion.1 = bf16[4,256,1152]{2,1,0:T(8,128)(2,1)} fusion(bf16[4,256,1152]{2,1,0:T(8,128)(2,1)} %scatter_fusion, s32[512]{0:T(512)S(1)} %get-tuple-element.150, bf16[512,1152]{1,0:T(8,128)(2,1)} %bitcast.207), kind=kCustom, calls=%fused_computation.6 | custom fusion | bytes 3543040 | tf_op jit(solution)/shard_map/scatter | solution.py:69
  897.7 11.4 psum.7
  909.7 55.2 %reduce-scatter.33.cloned.1.call-done = f32[144,864]{1,0:T(8,128)} async-done(((f32[1152,864]{1,0:T(8,128)}), f32[144,864]{1,0:T(8,128)}) %reduce-scatter.33.cloned.1.call-update) | async-done | bytes 497680
  979.2 11.0 all-gather.23.cloned.1.call-done
  992.7 80.0 %scatter_fusion.2 = f32[4,256,1152]{2,1,0:T(8,128)} fusion(f32[4,256,1152]{2,1,0:T(8,128)} %broadcast_in_dim.35, s32[512]{0:T(512)S(1)} %get-tuple-element.152, f32[512,1152]{1,0:T(8,128)} %bitcast.217), kind=kCustom, calls=%fused_computation.7 | custom fusion | bytes 7081984 | tf_op jit(solution)/shard_map/scatter | solution.py:69
  1072.7 79.7 %scatter_fusion.3 = f32[4,256,1152]{2,1,0:T(8,128)} fusion(f32[4,256,1152]{2,1,0:T(8,128)} %scatter_fusion.2, s32[512]{0:T(512)S(1)} %get-tuple-element.150, f32[512,1152]{1,0:T(8,128)} %bitcast.204), kind=kCustom, calls=%fused_computation.8 | custom fusion | bytes 7081984 | tf_op jit(solution)/shard_map/scatter | solution.py:69
  1152.4 21.2 %reduce-scatter.23.cloned.1.call-done = f32[144,6,288]{2,0,1:T(8,128)} async-done(((f32[1152,6,288]{2,0,1:T(8,128)}), f32[144,6,288]{2,0,1:T(8,128)}) %reduce-scatter.23.cloned.1.call-update) | async-done | bytes 995344 | tf_op jit(solution)/shard_map/reduce_scatter | solution.py:263
  (250 shorter events, 208.1 us)
Async XLA Ops:
  7.2 101.4 %all-gather.9.cloned.1.call-start = ((), (), s32[]{:S(2)}) async-start(), calls=%async_computation.10 | async-start | bytes 5971968 | tf_op jit(solution)/shard_map/all_gather | solution.py:111
  9.7 155.0 %all-gather.11.cloned.1.call-start = ((), (), s32[]{:S(2)}) async-start(), calls=%async_computation.11 | async-start | bytes 2985984 | tf_op jit(solution)/shard_map/all_gather | solution.py:112
  10.5 241.5 %reduce-scatter.15.cloned.1.call-start = ((), (), s32[]{:S(2)}) async-start(), calls=%async_computation.12 | async-start | bytes 2949120 | tf_op jit(solution)/shard_map/reduce_scatter | solution.py:73
  17.6 147.2 %copy-start.37 = (f32[4,128]{1,0:T(4,128)}, f32[4,128]{1,0:T(4,128)S(1)}, u32[]{:S(2)}) copy-start(f32[4,128]{1,0:T(4,128)S(1)} %broadcast_multiply_fusion.5) | copy-start | bytes 6148
  18.1 146.6 %copy-start.39 = (f32[4,128]{1,0:T(4,128)}, f32[4,128]{1,0:T(4,128)S(1)}, u32[]{:S(2)}) copy-start(f32[4,128]{1,0:T(4,128)S(1)} %add_rsqrt_fusion.1) | copy-start | bytes 6148
  172.8 99.0 %all-gather.13.cloned.1.call-start = ((), (), s32[]{:S(2)}) async-start(), calls=%async_computation.13 | async-start | bytes 1474560 | tf_op jit(solution)/shard_map/all_gather | solution.py:77
  174.7 11.3 collective-permute-start
  186.0 20.1 %collective-permute-start.1 = (bf16[144,1152]{1,0:T(8,128)(2,1)}, bf16[144,1152]{1,0:T(8,128)(2,1)}, u32[]{:S(2)}, u32[]{:S(2)}) collective-permute-start(bf16[144,1152]{1,0:T(8,128)(2,1)} %collective-permute-done), channel_id=1, source_target_pairs={{0,4},{4,8},{8,12},{12,16},{16,20},{20,24},{24,28},{28,0},{1,5},{5... | collective-permute-start | bytes 995336 | tf_op jit(solution)/shard_map/ppermute | solution.py:31
  186.0 24.4 %collective-permute-start.4 = (bf16[144,1152]{1,0:T(8,128)(2,1)}, bf16[144,1152]{1,0:T(8,128)(2,1)}, u32[]{:S(2)}, u32[]{:S(2)}) collective-permute-start(bf16[144,1152]{1,0:T(8,128)(2,1)} %convert_element_type.93), channel_id=1, source_target_pairs={{4,0},{8,4},{12,8},{16,12},{20,16},{24,20},{28,24},{0,28},{5,1},{9... | collective-permute-start | bytes 995336 | tf_op jit(solution)/shard_map/ppermute | solution.py:34
  206.1 14.9 %collective-permute-start.2 = (bf16[144,1152]{1,0:T(8,128)(2,1)}, bf16[144,1152]{1,0:T(8,128)(2,1)}, u32[]{:S(2)}, u32[]{:S(2)}) collective-permute-start(bf16[144,1152]{1,0:T(8,128)(2,1)} %collective-permute-done.1), channel_id=1, source_target_pairs={{0,4},{4,8},{8,12},{12,16},{16,20},{20,24},{24,28},{28,0},{1,5},{5... | collective-permute-start | bytes 995336 | tf_op jit(solution)/shard_map/ppermute | solution.py:31
  206.1 17.4 %copy-start.43 = (pred[4,128]{1,0:T(4,128)(4,1)S(1)}, pred[4,128]{1,0:T(4,128)(4,1)}, u32[]{:S(2)}) copy-start(pred[4,128]{1,0:T(4,128)(4,1)} %copy-done.42) | copy-start | bytes 1540
  210.4 16.5 %collective-permute-start.5 = (bf16[144,1152]{1,0:T(8,128)(2,1)}, bf16[144,1152]{1,0:T(8,128)(2,1)}, u32[]{:S(2)}, u32[]{:S(2)}) collective-permute-start(bf16[144,1152]{1,0:T(8,128)(2,1)} %collective-permute-done.4), channel_id=1, source_target_pairs={{4,0},{8,4},{12,8},{16,12},{20,16},{24,20},{28,24},{0,28},{5,1},{9... | collective-permute-start | bytes 995336 | tf_op jit(solution)/shard_map/ppermute | solution.py:34
  221.0 14.6 %collective-permute-start.3 = (bf16[144,1152]{1,0:T(8,128)(2,1)}, bf16[144,1152]{1,0:T(8,128)(2,1)}, u32[]{:S(2)}, u32[]{:S(2)}) collective-permute-start(bf16[144,1152]{1,0:T(8,128)(2,1)} %collective-permute-done.2), channel_id=1, source_target_pairs={{0,4},{4,8},{8,12},{12,16},{16,20},{20,24},{24,28},{28,0},{1,5},{5... | collective-permute-start | bytes 995336 | tf_op jit(solution)/shard_map/ppermute | solution.py:31
  226.9 33.8 %collective-permute-start.6 = (bf16[144,1152]{1,0:T(8,128)(2,1)}, bf16[144,1152]{1,0:T(8,128)(2,1)}, u32[]{:S(2)}, u32[]{:S(2)}) collective-permute-start(bf16[144,1152]{1,0:T(8,128)(2,1)} %collective-permute-done.5), channel_id=1, source_target_pairs={{4,0},{8,4},{12,8},{16,12},{20,16},{24,20},{28,24},{0,28},{5,1},{9... | collective-permute-start | bytes 995336 | tf_op jit(solution)/shard_map/ppermute | solution.py:34
  255.3 130.6 %reduce-scatter.29.cloned.1.call-start = ((), (), s32[]{:S(2)}) async-start(), calls=%async_computation.25 | async-start | bytes 5971968 | tf_op jit(solution)/shard_map/reduce_scatter | solution.py:267
  281.5 162.8 %all-gather.15.cloned.1.call-start = ((), (), s32[]{:S(2)}) async-start(), calls=%async_computation.14 | async-start | bytes 2985984 | tf_op jit(solution)/shard_map/all_gather | solution.py:115
  389.4 111.3 %all-gather.19.cloned.1.call-start = ((), (), s32[]{:S(2)}) async-start(), calls=%async_computation.17 | async-start | bytes 2985984 | tf_op jit(solution)/shard_map/all_gather | solution.py:178
  390.1 147.8 %reduce-scatter.19.cloned.1.call-start = ((), (), s32[]{:S(2)}) async-start(), calls=%async_computation.18 | async-start | bytes 2949120 | tf_op jit(solution)/shard_map/reduce_scatter | solution.py:73
  506.2 67.6 %reduce-scatter.17.cloned.1.call-start = ((), (), s32[]{:S(2)}) async-start(), calls=%async_computation.15 | async-start | bytes 2949120 | tf_op jit(solution)/shard_map/reduce_scatter | solution.py:73
  512.3 84.1 %all-gather.21.cloned.1.call-start = ((), (), s32[]{:S(2)}) async-start(), calls=%async_computation.19 | async-start | bytes 1474560 | tf_op jit(solution)/shard_map/all_gather | solution.py:77
  578.8 59.6 %reduce-scatter.21.cloned.1.call-start = ((), (), s32[]{:S(2)}) async-start(), calls=%async_computation.20 | async-start | bytes 2949120 | tf_op jit(solution)/shard_map/reduce_scatter | solution.py:73
  605.2 87.7 %reduce-scatter.31.cloned.1.call-start = ((), (), s32[]{:S(2)}) async-start(), calls=%async_computation.26 | async-start | bytes 737280
  655.0 74.8 %all-gather.17.cloned.1.call-start = ((), (), s32[]{:S(2)}) async-start(), calls=%async_computation.16 | async-start | bytes 1474560 | tf_op jit(solution)/shard_map/all_gather | solution.py:77
  655.7 233.0 %reduce-scatter.25.cloned.1.call-start = ((), (), s32[]{:S(2)}) async-start(), calls=%async_computation.23 | async-start | bytes 1990656 | tf_op jit(solution)/shard_map/reduce_scatter | solution.py:265
  659.2 231.4 %reduce-scatter.27.cloned.1.call-start = ((), (), s32[]{:S(2)}) async-start(), calls=%async_computation.24 | async-start | bytes 5971968 | tf_op jit(solution)/shard_map/reduce_scatter | solution.py:266
  665.0 299.9 %reduce-scatter.33.cloned.1.call-start = ((), (), s32[]{:S(2)}) async-start(), calls=%async_computation.27 | async-start | bytes 4644864
  688.0 302.2 %all-gather.23.cloned.1.call-start = ((), (), s32[]{:S(2)}) async-start(), calls=%async_computation.21 | async-start | bytes 2949120 | tf_op jit(solution)/shard_map/all_gather | solution.py:242
  692.3 481.3 %reduce-scatter.23.cloned.1.call-start = ((), (), s32[]{:S(2)}) async-start(), calls=%async_computation.22 | async-start | bytes 11943936 | tf_op jit(solution)/shard_map/reduce_scatter | solution.py:263
  809.9 78.8 %copy-start.23 = (f32[288,144]{0,1:T(8,128)S(1)}, f32[288,144]{0,1:T(8,128)}, u32[]{:S(2)}) copy-start(f32[288,144]{0,1:T(8,128)} %param.33) | copy-start | bytes 497668
  809.9 78.8 %copy-start.30 = (f32[288,144]{0,1:T(8,128)S(1)}, f32[288,144]{0,1:T(8,128)}, u32[]{:S(2)}) copy-start(f32[288,144]{0,1:T(8,128)} %param.43) | copy-start | bytes 497668
  809.9 80.7 %copy-start.6 = (f32[144,1152]{1,0:T(8,128)S(1)}, f32[144,1152]{1,0:T(8,128)}, u32[]{:S(2)}) copy-start(f32[144,1152]{1,0:T(8,128)} %param.34) | copy-start | bytes 1990660
  897.7 72.1 %copy-start.10 = (f32[3,144,288]{1,2,0:T(8,128)S(1)}, f32[3,144,288]{1,2,0:T(8,128)}, u32[]{:S(2)}) copy-start(f32[3,144,288]{1,2,0:T(8,128)} %copy.131) | copy-start | bytes 1492996
  (42 other events, 111.0 us)
Sparse Core Ops, SparseCore 0:
  10.9 97.6 all-gather.8
  111.4 53.2 all-gather.10
  172.9 31.6 reduce-scatter.14
  255.4 16.3 all-gather.12
  281.7 104.1 reduce-scatter.28
  389.5 54.7 all-gather.14
  447.1 53.5 all-gather.18
  506.3 31.6 reduce-scatter.18
  540.6 33.0 reduce-scatter.16
  578.9 17.4 all-gather.20
  605.3 33.0 reduce-scatter.20
  655.1 22.0 reduce-scatter.30
  679.4 17.4 all-gather.16
  700.6 66.5 reduce-scatter.24
  770.6 103.0 reduce-scatter.26
  877.5 87.3 reduce-scatter.32
  966.3 23.8 all-gather.22
  993.6 179.9 reduce-scatter.22
